TPU v7x, 256 devices: a whole 4x4x8 slice. The times are simulated.
256 devices in a mesh: group: 32 (over x, z), local: 4 (over y), rep: 2 (over core).
Axes of the slice: x: 4, y: 4, z: 8, core: 2. Of those that a mesh axis runs over, the one named last changes fastest.
Arguments:
- tokens: bfloat16 [16384, 2560], P(('rep', 'group', 'local')), parts along dimension 0, may hold values from -6 to 6
- gates: bfloat16 [16384, 8], P(('rep', 'group', 'local')), parts along dimension 0, may hold values from 0.049804688 to 1
- expert_ids: int32 [16384, 8], P(('rep', 'group', 'local')), parts along dimension 0, may hold values from 0 to 127, as said below
- w_gate: bfloat16 [128, 2560, 768], P(('group', 'local')), may hold values from -0.125 to 0.125
- w_up: bfloat16 [128, 2560, 768], P(('group', 'local')), may hold values from -0.125 to 0.125
- w_down: bfloat16 [128, 768, 2560], P(('group', 'local')), may hold values from -0.21875 to 0.21875
Outputs:
- mixed: bfloat16 [16384, 2560], P(('rep', 'group', 'local')), parts along dimension 0
There are 2 independent parts, one for each index of `rep`. A program takes and returns all parts, laid end to end along the dimension named above; an argument that names none is the same for every part. Nothing has to cross between parts.
Inputs may be any that keep to these rules, and one draw needn't show every extreme that they name: `expert_ids`: each row names 8 different experts, which lie in at most 4 groups (expert // 4).
All inputs are finite; a program needn't handle non-finite values.
Results may differ from a plain program's by a relative error of at most 0.0057.
Values may be sent and summed in bfloat16 or wider, within the bound.
A program may use at most 64 MiB of HBM per device.

v0:
```python
import jax
import jax.numpy as jnp
from jax import lax
from jax.sharding import PartitionSpec as P

GROUPS_TOK = 4


def expert_rows(rows, gate_mat, up_mat, down_mat):
    gate = jnp.dot(rows, gate_mat, preferred_element_type=jnp.float32)
    up = jnp.dot(rows, up_mat, preferred_element_type=jnp.float32)
    hidden = (jax.nn.silu(gate) * up).astype(jnp.bfloat16)
    return jnp.dot(hidden, down_mat, preferred_element_type=jnp.float32).astype(jnp.bfloat16)


def shards(tokens, gates, expert_ids, w_gate, w_up, w_down):
    tok_rows, width = tokens.shape
    n_group = lax.axis_size("group")
    local_expert_count = lax.axis_size("local")
    capacity = min(tok_rows, tok_rows * GROUPS_TOK // n_group)
    expert_iota = jnp.arange(n_group * local_expert_count, dtype=jnp.int32)
    hits = expert_ids[:, :, None] == expert_iota
    weights = jnp.sum(
        jnp.where(hits, gates.astype(jnp.float32)[:, :, None], jnp.float32(0.0)), axis=1
    )
    member = jnp.any(
        jnp.any(hits, axis=1).reshape(tok_rows, n_group, local_expert_count), axis=2
    ).astype(jnp.int32)
    rank = jnp.cumsum(member, axis=0) - member
    slot_iota = jnp.arange(capacity, dtype=jnp.int32)
    place = (member[:, :, None] == 1) & (rank[:, :, None] == slot_iota)
    place_f = place.astype(jnp.float32)
    outgoing = jnp.einsum(
        "tgc,td->gcd", place.astype(jnp.bfloat16), tokens, preferred_element_type=jnp.float32
    ).astype(jnp.bfloat16)
    slot_weights = jnp.einsum(
        "tgc,tgl->gcl",
        place_f,
        weights.reshape(tok_rows, n_group, local_expert_count),
        precision=lax.Precision.HIGHEST,
    ).astype(jnp.bfloat16)
    send_rows = jnp.broadcast_to(
        outgoing[:, None], (n_group, local_expert_count, capacity, width)
    ).reshape(n_group * local_expert_count, capacity, width)
    send_weights = jnp.transpose(slot_weights, (0, 2, 1)).reshape(
        n_group * local_expert_count, capacity
    )
    received_rows, got_weights = (
        lax.all_to_all(send_rows, ("group", "local"), split_axis=0, concat_axis=0, tiled=True),
        lax.all_to_all(send_weights, ("group", "local"), split_axis=0, concat_axis=0, tiled=True),
    )
    arrived = received_rows.reshape(n_group, local_expert_count, capacity, width)
    own_weights = got_weights.reshape(n_group, local_expert_count, capacity)
    outputs = expert_rows(
        arrived.reshape(n_group * local_expert_count * capacity, width),
        w_gate[0],
        w_up[0],
        w_down[0],
    )
    outputs = outputs.reshape(n_group, local_expert_count, capacity, width)
    masked = jnp.where(own_weights[..., None] > 0, outputs, jnp.zeros_like(outputs))
    returned_rows = lax.all_to_all(
        masked.reshape(n_group * local_expert_count, capacity, width),
        ("group", "local"),
        split_axis=0,
        concat_axis=0,
        tiled=True,
    )
    returned_rows = returned_rows.reshape(n_group, local_expert_count, capacity, width)
    sender_weights = jnp.transpose(slot_weights, (0, 2, 1))
    combined = jnp.einsum(
        "zqa,zqap->zap", sender_weights, returned_rows, preferred_element_type=jnp.float32
    )
    mixed = jnp.einsum("tgc,gcd->td", place_f, combined, precision=lax.Precision.HIGHEST)
    return mixed.astype(jnp.bfloat16)


def solution(mesh):
    in_specs = (
        P(("rep", "group", "local"), None),
        P(("rep", "group", "local"), None),
        P(("rep", "group", "local"), None),
        P(("group", "local"), None, None),
        P(("group", "local"), None, None),
        P(("group", "local"), None, None),
    )
    out_specs = P(("rep", "group", "local"), None)
    return jax.shard_map(shards, mesh=mesh, in_specs=in_specs, out_specs=out_specs, check_vma=False)
```

profile of v0, /device:TPU:2, one launch (start us, length us, event | category | flops | bytes accessed | tf_op | source)
XLA Modules:
  0.0 314.5 jit_solution(18292289938177435894)
XLA Ops:
  0.0 0.0 copy-start
  0.0 0.8 copy.49
  0.8 0.2 fusion.17
  1.0 0.1 copy.50
  1.1 0.1 reduce_or.19
  1.2 0.1 copy.51
  1.3 0.1 reduce_window_sum.11
  1.4 0.1 copy.53
  1.5 0.1 copy.52
  1.6 0.8 copy.54
  2.3 0.2 select_reduce_fusion
  2.6 0.1 copy.55
  2.7 0.2 convolution_convert_fusion.2
  2.9 0.7 copy.57
  3.6 15.5 %all-to-all-start = ((bf16[128,1,8]{2,1,0:T(2,128)(2,1)}), bf16[128,1,8]{2,1,0:T(2,128)(2,1)S(1)}, u32[]{:S(2)}, u32[]{:S(2)}) async-start(bf16[128,1,8]{2,1,0:T(2,128)(2,1)} %copy.57), calls=%async_computation | async-start | bytes 131072 | tf_op jit(solution)/shard_map/all_to_all | solution.py:50
  19.2 0.0 copy-done
  19.2 0.5 convolution_convert_fusion.1
  19.7 10.3 %all-to-all-done = bf16[128,1,8]{2,1,0:T(2,128)(2,1)S(1)} async-done(((bf16[128,1,8]{2,1,0:T(2,128)(2,1)}), bf16[128,1,8]{2,1,0:T(2,128)(2,1)S(1)}, u32[]{:S(2)}, u32[]{:S(2)}) %all-to-all-start) | async-done | bytes 2080 | tf_op jit(solution)/shard_map/all_to_all | solution.py:50
  30.0 2.7 broadcast_in_dim.38
  32.7 8.1 %all-to-all-start.1 = ((bf16[128,8,2560]{2,1,0:T(8,128)(2,1)}), bf16[128,8,2560]{2,1,0:T(8,128)(2,1)}, u32[]{:S(2)}, u32[]{:S(2)}) async-start(bf16[128,8,2560]{2,1,0:T(8,128)(2,1)} %bitcast.41), calls=%async_computation.1 | async-start | bytes 10485760 | tf_op jit(solution)/shard_map/all_to_all | solution.py:49
  40.9 0.1 copy.58
  40.9 0.1 copy.59
  41.1 117.3 %all-to-all-done.1 = bf16[128,8,2560]{2,1,0:T(8,128)(2,1)} async-done(((bf16[128,8,2560]{2,1,0:T(8,128)(2,1)}), bf16[128,8,2560]{2,1,0:T(8,128)(2,1)}, u32[]{:S(2)}, u32[]{:S(2)}) %all-to-all-start.1) | async-done | bytes 5242912 | tf_op jit(solution)/shard_map/all_to_all | solution.py:49
  158.4 7.5 %fusion = f32[1024,768]{1,0:T(8,128)S(1)} fusion(bf16[128,8,2560]{2,1,0:T(8,128)(2,1)} %all-to-all-done.1, bf16[1,2560,768]{2,1,0:T(8,128)(2,1)} %param.10), kind=kOutput, calls=%fused_computation.2 | convolution fusion | flops 4026531840 | bytes 12320768 | tf_op jit(solution)/shard_map/dot_general | solution.py:11
  165.9 0.0 copy-start.2
  165.9 7.2 %multiply_convert_fusion = bf16[1024,768]{1,0:T(8,128)(2,1)S(1)} fusion(f32[1024,768]{1,0:T(8,128)S(1)} %fusion, bf16[1,2560,768]{2,1,0:T(8,128)(2,1)S(1)} %copy-done.1, bf16[128,8,2560]{2,1,0:T(8,128)(2,1)} %all-to-all-done.1), kind=kOutput, calls=%fused_computation.14 | convolution fusion | flops 4031250432 | bytes 13893632 | tf_op jit(solution)/shard_map/dot_general | solution.py:10
  173.1 6.1 %bitcast_select_fusion = bf16[128,8,2560]{2,1,0:T(8,128)(2,1)} fusion(pred[128,8]{1,0:T(8,128)(4,1)S(1)} %copy.59, bf16[1024,768]{1,0:T(8,128)(2,1)S(1)} %multiply_convert_fusion, bf16[1,768,2560]{2,1,0:T(8,128)(2,1)S(1)} %copy-done.2), kind=kOutput, calls=%fused_computation.1 | convolution fusion | flops 4031774720 | bytes 10748928 | tf_op jit(solution)/shard_map/dot_general | solution.py:13
  179.2 8.6 %all-to-all-start.2 = ((bf16[128,8,2560]{2,1,0:T(8,128)(2,1)}), bf16[128,8,2560]{2,1,0:T(8,128)(2,1)}, u32[]{:S(2)}, u32[]{:S(2)}) async-start(bf16[128,8,2560]{2,1,0:T(8,128)(2,1)} %bitcast_select_fusion), calls=%async_computation.2 | async-start | bytes 10485760 | tf_op jit(solution)/shard_map/all_to_all | solution.py:62
  187.8 0.3 copy.61
  188.1 117.6 %all-to-all-done.2 = bf16[128,8,2560]{2,1,0:T(8,128)(2,1)} async-done(((bf16[128,8,2560]{2,1,0:T(8,128)(2,1)}), bf16[128,8,2560]{2,1,0:T(8,128)(2,1)}, u32[]{:S(2)}, u32[]{:S(2)}) %all-to-all-start.2) | async-done | bytes 5242912 | tf_op jit(solution)/shard_map/all_to_all | solution.py:62
  305.7 5.4 %fusion.4 = f32[32,8,1,2560]{3,2,1,0:T(1,128)S(1)} fusion(bf16[32,4,8,1]{1,3,2,0:T(2,128)(2,1)S(1)} %copy.61, bf16[32,4,8,2560]{3,2,1,0:T(8,128)(2,1)} %bitcast.12), kind=kOutput, calls=%fused_computation.6 | convolution fusion | flops 5242880 | bytes 7866368 | tf_op jit(solution)/shard_map/zqa,zqap->zap/dot_general | solution.py:71
  311.1 3.4 %fusion.9 = bf16[64,2560]{1,0:T(8,128)(2,1)} fusion(f32[32,8,1,2560]{3,2,1,0:T(1,128)S(1)} %fusion.4, s32[64,32]{0,1:T(8,128)S(1)} %copy.53, pred[64,32]{0,1:T(8,128)(4,1)S(1)} %copy.52), kind=kOutput, calls=%fused_computation.13 | convolution fusion | flops 503513088 | bytes 2959360 | tf_op jit(solution)/shard_map/tgc,gcd->td/dot_general | solution.py:74
  (7 shorter events, 0.1 us)
Async XLA Ops:
  0.0 19.2 %copy-start = (bf16[64,2560]{1,0:T(8,128)(2,1)S(1)}, bf16[64,2560]{1,0:T(8,128)(2,1)}, u32[]{:S(2)}) copy-start(bf16[64,2560]{1,0:T(8,128)(2,1)} %param.6) | copy-start | bytes 983044
  3.6 26.4 %all-to-all-start = ((bf16[128,1,8]{2,1,0:T(2,128)(2,1)}), bf16[128,1,8]{2,1,0:T(2,128)(2,1)S(1)}, u32[]{:S(2)}, u32[]{:S(2)}) async-start(bf16[128,1,8]{2,1,0:T(2,128)(2,1)} %copy.57), calls=%async_computation | async-start | bytes 131072 | tf_op jit(solution)/shard_map/all_to_all | solution.py:50
  32.7 125.7 %all-to-all-start.1 = ((bf16[128,8,2560]{2,1,0:T(8,128)(2,1)}), bf16[128,8,2560]{2,1,0:T(8,128)(2,1)}, u32[]{:S(2)}, u32[]{:S(2)}) async-start(bf16[128,8,2560]{2,1,0:T(8,128)(2,1)} %bitcast.41), calls=%async_computation.1 | async-start | bytes 10485760 | tf_op jit(solution)/shard_map/all_to_all | solution.py:49
  158.4 7.5 %copy-start.1 = (bf16[1,2560,768]{2,1,0:T(8,128)(2,1)S(1)}, bf16[1,2560,768]{2,1,0:T(8,128)(2,1)}, u32[]{:S(2)}) copy-start(bf16[1,2560,768]{2,1,0:T(8,128)(2,1)} %param.9) | copy-start | bytes 11796484
  165.9 7.2 %copy-start.2 = (bf16[1,768,2560]{2,1,0:T(8,128)(2,1)S(1)}, bf16[1,768,2560]{2,1,0:T(8,128)(2,1)}, u32[]{:S(2)}) copy-start(bf16[1,768,2560]{2,1,0:T(8,128)(2,1)} %param.11) | copy-start | bytes 11796484
  179.2 126.6 %all-to-all-start.2 = ((bf16[128,8,2560]{2,1,0:T(8,128)(2,1)}), bf16[128,8,2560]{2,1,0:T(8,128)(2,1)}, u32[]{:S(2)}, u32[]{:S(2)}) async-start(bf16[128,8,2560]{2,1,0:T(8,128)(2,1)} %bitcast_select_fusion), calls=%async_computation.2 | async-start | bytes 10485760 | tf_op jit(solution)/shard_map/all_to_all | solution.py:62
where the time goes:
time: 315 us
  waiting for transfers between devices  245 us (78%)
  starting transfers between devices  32.3 us (10%)
  matrix products  30.2 us (10%)
  local copies, waits for them, and re-layouts  6 us (2%)
    all_to_all x1, waiting for transfers between devices, shards(): lax.all_to_all(masked.reshape(n_group * local_expert_count, capacity, wid...  118 us
    all_to_all x1, waiting for transfers between devices, shards(): lax.all_to_all(send_rows, ('group', 'local'), split_axis=0, concat_axis=0...  117 us
    all_to_all x1, starting transfers between devices, shards(): lax.all_to_all(send_weights, ('group', 'local'), split_axis=0, concat_axi...  15.5 us
    all_to_all x1, waiting for transfers between devices, shards(): lax.all_to_all(send_weights, ('group', 'local'), split_axis=0, concat_axi...  10.3 us
    all_to_all x1, starting transfers between devices, shards(): lax.all_to_all(masked.reshape(n_group * local_expert_count, capacity, wid...  8.64 us
    all_to_all x1, starting transfers between devices, shards(): lax.all_to_all(send_rows, ('group', 'local'), split_axis=0, concat_axis=0...  8.13 us
    dot_general x1, matrix products, expert_rows(): up = jnp.dot(rows, up_mat, preferred_element_type=jnp.float32)  7.46 us
    dot_general x1, matrix products, expert_rows(): gate = jnp.dot(rows, gate_mat, preferred_element_type=jnp.float32)  7.19 us
  transfers between devices with their start and end apart: 3, of which 3 were waited for; matrix products, arithmetic and copies ran while one was open for 0% of the time, Pallas kernels for 0%

commit v1 on v0

v1 whole, which is shorter than its diff:
```python
import functools

import jax
import jax.numpy as jnp
from jax import lax
from jax.experimental import pallas as pl
from jax.experimental.pallas import tpu as pltpu
from jax.sharding import PartitionSpec as P

MESH = pl.DeviceIdType.MESH
GROUPS_TOK = 4
RING_Z = 8
LANES = 128
BLOCKS_CHUNK = 8


def tile_of(size, most):
    tile = min(size, most)
    while size % tile:
        tile -= LANES
    return tile


def layer_kernel(
    cfg,
    tok_ref, ids_ref, gates_ref, wg_hbm, wu_hbm, wd_hbm,
    out_ref,
    wg, wu, wd, sent, place_ref, rows, wcol, hidden, part, half_in, full_in, back, returned,
    w_sem, a_send, a_recv, d_send, d_recv, f_send, f_recv, p_send, p_recv, q_send, q_recv, b_send, b_recv,
):
    n_group, cap, nz, nb, chunks, width, ff = cfg
    nx = n_group // nz
    n_tok = tok_ref.shape[0]
    part_rows = nb * cap
    half = part_rows // 2
    slots = n_group * cap
    f32, bf16 = jnp.float32, jnp.bfloat16

    me = lax.axis_index("group")
    mx, mz = me // nz, lax.rem(me, nz)
    my = lax.axis_index("local")
    right, left = lax.rem(my + 1, 4), lax.rem(my + 3, 4)

    def forth(j):
        return lax.rem(mx + j // nz, nx) * nz + lax.rem(mz + lax.rem(j, nz), nz)

    def origin(j):
        return lax.rem(mx + nx - j // nz, nx) * nz + lax.rem(mz + nz - lax.rem(j, nz), nz)

    barrier = pltpu.get_barrier_semaphore()

    def greet(j, carry):
        pl.semaphore_signal(barrier, inc=1, device_id={"group": forth(j)}, device_id_type=MESH)
        return carry

    lax.fori_loop(1, n_group, greet, 0)
    pl.semaphore_signal(barrier, inc=1, device_id={"local": right}, device_id_type=MESH)
    pl.semaphore_signal(barrier, inc=1, device_id={"local": left}, device_id_type=MESH)

    loads = [
        pltpu.make_async_copy(hbm.at[0], vmem, w_sem.at[i])
        for i, (hbm, vmem) in enumerate(((wg_hbm, wg), (wu_hbm, wu), (wd_hbm, wd)))
    ]
    for load in loads:
        load.start()

    expert_at = lax.broadcasted_iota(jnp.int32, (LANES, n_tok), 0)
    hit = jnp.zeros((LANES, n_tok), f32)
    weight = jnp.zeros((LANES, n_tok), f32)
    for k in range(ids_ref.shape[0]):
        same = ids_ref[k : k + 1, :] == expert_at
        hit = jnp.where(same, 1.0, hit)
        weight = jnp.where(same, gates_ref[k : k + 1, :].astype(f32), weight)
    slot_at = lax.broadcasted_iota(jnp.int32, (slots, LANES), 0)
    of_expert = lax.broadcasted_iota(jnp.int32, (slots, LANES), 1)
    in_group = jnp.where(slot_at // cap == of_expert // 4, 1.0, 0.0).astype(bf16)
    count = jnp.dot(in_group, hit.astype(bf16), preferred_element_type=f32)
    member = jnp.where(count > 0.5, 1.0, 0.0)
    t_row = lax.broadcasted_iota(jnp.int32, (n_tok, n_tok), 0)
    t_col = lax.broadcasted_iota(jnp.int32, (n_tok, n_tok), 1)
    before = jnp.where(t_row < t_col, 1.0, 0.0).astype(bf16)
    rank = jnp.dot(member.astype(bf16), before, preferred_element_type=f32)
    slot_rank = lax.rem(lax.broadcasted_iota(jnp.int32, (slots, n_tok), 0), cap).astype(f32)
    place = jnp.where((count > 0.5) & (rank == slot_rank), 1.0, 0.0).astype(bf16)
    across = (((1,), (1,)), ((), ()))
    same_tok = jnp.where(t_row == t_col, 1.0, 0.0).astype(bf16)
    place_ref[...] = lax.dot_general(same_tok, place, across, preferred_element_type=f32).astype(bf16)
    sent[:, width:] = lax.dot_general(
        place, weight.astype(bf16), across, preferred_element_type=f32
    ).astype(bf16)
    cols = tile_of(width, 512)

    def gather_cols(n, carry):
        at = pl.ds(pl.multiple_of(n * cols, cols), cols)
        sent[:, at] = jnp.dot(place, tok_ref[:, at], preferred_element_type=f32).astype(bf16)
        return carry

    lax.fori_loop(0, width // cols, gather_cols, 0)
    pl.semaphore_wait(barrier, n_group + 1)

    def block(ref, index):
        return ref.at[pl.ds(pl.multiple_of(index * cap, cap), cap), :]

    def dispatch(j):
        target = forth(j)
        return pltpu.make_async_remote_copy(
            src_ref=block(sent, target),
            dst_ref=block(rows.at[j // nb], lax.rem(j, nb)),
            send_sem=a_send.at[j],
            recv_sem=a_recv.at[j],
            device_id={"group": target},
            device_id_type=MESH,
        )

    def give_back(j):
        return pltpu.make_async_remote_copy(
            src_ref=block(back.at[j // nb], lax.rem(j, nb)),
            dst_ref=block(returned, me),
            send_sem=b_send.at[j],
            recv_sem=b_recv.at[j],
            device_id={"group": origin(j)},
            device_id_type=MESH,
        )

    own_in = pltpu.make_async_copy(block(sent, me), rows.at[0, pl.ds(0, cap), :], a_recv.at[0])
    own_in.start()

    def start_dispatch(j, carry):
        dispatch(j).start()
        return carry

    lax.fori_loop(1, n_group, start_dispatch, 0)

    def copy_y(src, dst, send, recv, side):
        return pltpu.make_async_remote_copy(
            src_ref=src, dst_ref=dst, send_sem=send, recv_sem=recv,
            device_id={"local": right if side == 0 else left}, device_id_type=MESH,
        )

    def piece(ref, c, begin, size):
        return ref.at[c, pl.ds(begin, size), :]

    n1, n2, n3 = part_rows, 2 * part_rows, 3 * part_rows

    def direct(c, side):
        return copy_y(piece(rows, c, 0, n1), piece(rows, c, (n3, n1)[side], n1),
                      d_send.at[c, side], d_recv.at[c, side], side)

    def onward(c, side):
        return copy_y(piece(rows, c, (n3, n1 + half)[side], half), piece(rows, c, (n2, n2 + half)[side], half),
                      f_send.at[c, side], f_recv.at[c, side], side)

    def far(c, side):
        return copy_y(piece(part, c, (n2, n2 + half)[side], half), half_in.at[c, side],
                      p_send.at[c, side], p_recv.at[c, side], side)

    def near(c, side, which):
        begin = (half if which == 0 else 0) if side == 0 else (0 if which == 0 else half)
        return copy_y(piece(part, c, (n1, n3)[side] + begin, half), full_in.at[c, side, pl.ds(begin, half), :],
                      q_send.at[c, 2 * which + side], q_recv.at[c, 2 * which + side], side)

    fcols = tile_of(ff, 256)
    dcols = tile_of(width, 512)

    def compute(c):
        lane = lax.broadcasted_iota(jnp.int32, (4 * part_rows, LANES), 1)
        gate_of = rows[c, :, width:].astype(f32)
        mine = jnp.sum(jnp.where(lane == me * 4 + my, gate_of, 0.0), axis=1, keepdims=True)
        wcol[...] = jnp.broadcast_to(mine, (4 * part_rows, LANES))

        def up_cols(n, carry):
            at = pl.ds(pl.multiple_of(n * fcols, fcols), fcols)
            x = rows[c, :, :width]
            gate = jnp.dot(x, wg[:, at], preferred_element_type=f32)
            up = jnp.dot(x, wu[:, at], preferred_element_type=f32)
            hidden[:, at] = (gate / (1.0 + jnp.exp(-gate)) * up).astype(bf16)
            return carry

        lax.fori_loop(0, ff // fcols, up_cols, 0)

        def down_cols(n, carry):
            at = pl.ds(pl.multiple_of(n * dcols, dcols), dcols)
            value = jnp.dot(hidden[...], wd[:, at], preferred_element_type=f32)
            part[c, :, at] = (value * wcol[:, 0:1]).astype(bf16)
            return carry

        lax.fori_loop(0, width // dcols, down_cols, 0)

    def step(s, carry):
        @pl.when(s < chunks)
        def _():
            c = s

            def arrived(b, inner):
                j = c * nb + b
                pltpu.make_async_copy(block(sent, 0), block(rows.at[c], b), a_recv.at[j]).wait()
                return inner

            lax.fori_loop(0, nb, arrived, 0)
            direct(c, 0).start()
            direct(c, 1).start()

        @pl.when((s >= 1) & (s <= chunks))
        def _():
            c = s - 1
            for side in (0, 1):
                direct(c, side).wait_recv()
                onward(c, side).start()

        @pl.when((s >= 2) & (s <= chunks + 1))
        def _():
            c = s - 2

            @pl.when(c == 0)
            def _():
                for load in loads:
                    load.wait()

            for side in (0, 1):
                onward(c, side).wait_recv()
            compute(c)
            for side in (0, 1):
                far(c, side).start()
            for side in (0, 1):
                near(c, side, 0).start()

        @pl.when((s >= 3) & (s <= chunks + 2))
        def _():
            c = s - 3
            for side in (0, 1):
                far(c, side).wait_recv()
                at = pl.ds((n1, n3 + half)[side], half)
                part[c, at, :] = (part[c, at, :].astype(f32) + half_in[c, side].astype(f32)).astype(bf16)
                near(c, side, 1).start()

        @pl.when(s >= 4)
        def _():
            c = s - 4
            for which in (0, 1):
                for side in (0, 1):
                    near(c, side, which).wait_recv()
            back[c] = (
                part[c, pl.ds(0, n1), :].astype(f32)
                + full_in[c, 0].astype(f32)
                + full_in[c, 1].astype(f32)
            ).astype(bf16)

            def send_back(b, inner):
                j = c * nb + b

                @pl.when(j == 0)
                def _():
                    pltpu.make_async_copy(block(back.at[0], 0), block(returned, me), b_recv.at[0]).start()

                @pl.when(j != 0)
                def _():
                    give_back(j).start()

                return inner

            lax.fori_loop(0, nb, send_back, 0)

        return carry

    lax.fori_loop(0, chunks + 4, step, 0)

    def sends_done(c, carry):
        for side in (0, 1):
            direct(c, side).wait_send()
            onward(c, side).wait_send()
            far(c, side).wait_send()
            near(c, side, 0).wait_send()
            near(c, side, 1).wait_send()
        return carry

    lax.fori_loop(0, chunks, sends_done, 0)

    def blocks_done(j, carry):
        dispatch(j).wait_send()
        give_back(j).wait_send()
        return carry

    lax.fori_loop(1, n_group, blocks_done, 0)

    def came_back(j, carry):
        pltpu.make_async_copy(block(back.at[0], 0), block(returned, forth(j)), b_recv.at[j]).wait()
        return carry

    lax.fori_loop(0, n_group, came_back, 0)

    def mix_cols(n, carry):
        at = pl.ds(pl.multiple_of(n * cols, cols), cols)
        out_ref[:, at] = jnp.dot(place_ref[...], returned[:, at], preferred_element_type=f32).astype(bf16)
        return carry

    lax.fori_loop(0, width // cols, mix_cols, 0)


def shards(ring_z, blocks_chunk, tokens, gates, expert_ids, w_gate, w_up, w_down):
    n_tok, width = tokens.shape
    n_group = lax.axis_size("group")
    ff = w_gate.shape[2]
    cap = min(n_tok, n_tok * GROUPS_TOK // n_group)
    nb = blocks_chunk
    chunks = n_group // nb
    n1 = nb * cap
    bf16 = jnp.bfloat16
    vmem = pl.BlockSpec(memory_space=pltpu.VMEM)
    hbm = pl.BlockSpec(memory_space=pl.ANY)
    dma = pltpu.SemaphoreType.DMA
    cfg = (n_group, cap, ring_z, nb, chunks, width, ff)
    return pl.pallas_call(
        functools.partial(layer_kernel, cfg),
        out_shape=jax.ShapeDtypeStruct((n_tok, width), bf16),
        in_specs=[vmem, vmem, vmem, hbm, hbm, hbm],
        out_specs=vmem,
        scratch_shapes=[
            pltpu.VMEM((width, ff), bf16),
            pltpu.VMEM((width, ff), bf16),
            pltpu.VMEM((ff, width), bf16),
            pltpu.VMEM((n_group * cap, width + LANES), bf16),
            pltpu.VMEM((n_tok, n_group * cap), bf16),
            pltpu.VMEM((chunks, 4 * n1, width + LANES), bf16),
            pltpu.VMEM((4 * n1, LANES), jnp.float32),
            pltpu.VMEM((4 * n1, ff), bf16),
            pltpu.VMEM((chunks, 4 * n1, width), bf16),
            pltpu.VMEM((chunks, 2, n1 // 2, width), bf16),
            pltpu.VMEM((chunks, 2, n1, width), bf16),
            pltpu.VMEM((chunks, n1, width), bf16),
            pltpu.VMEM((n_group * cap, width), bf16),
            dma((3,)),
            dma((n_group,)), dma((n_group,)),
            dma((chunks, 2)), dma((chunks, 2)),
            dma((chunks, 2)), dma((chunks, 2)),
            dma((chunks, 2)), dma((chunks, 2)),
            dma((chunks, 4)), dma((chunks, 4)),
            dma((n_group,)), dma((n_group,)),
        ],
        compiler_params=pltpu.CompilerParams(
            collective_id=0, has_side_effects=True, vmem_limit_bytes=60 * 1024 * 1024
        ),
        name="moe_layer",
    )(tokens, expert_ids.T, gates.T, w_gate, w_up, w_down)


def solution(mesh):
    in_specs = (
        P(("rep", "group", "local"), None),
        P(("rep", "group", "local"), None),
        P(("rep", "group", "local"), None),
        P(("group", "local"), None, None),
        P(("group", "local"), None, None),
        P(("group", "local"), None, None),
    )
    out_specs = P(("rep", "group", "local"), None)
    return jax.shard_map(
        functools.partial(shards, RING_Z, BLOCKS_CHUNK),
        mesh=mesh, in_specs=in_specs, out_specs=out_specs, check_vma=False,
    )
```

time: 315 us -> 127 us (0.40)
  waiting for transfers between devices: 245 us -> 0 us
  Pallas kernels: 0 us -> 125 us
  starting transfers between devices: 32.3 us -> 0 us
  matrix products: 30.2 us -> 0 us
  local copies, waits for them, and re-layouts: 6 us -> 1.72 us
    all_to_all x3 -> x0, waiting for transfers between devices: 245 us -> none  [the longest x1 118 us: shards(): lax.all_to_all(masked.reshape(n_group * local_expert_count, capacity, wid...]
    pallas_call x0 -> x1, Pallas kernels: none -> 125 us  [shards(): pl.pallas_call(functools.partial(layer_kernel, cfg), out_shape=jax.ShapeD...]
    all_to_all x3 -> x0, starting transfers between devices: 32.3 us -> none  [the longest x1 15.5 us: shards(): lax.all_to_all(send_weights, ('group', 'local'), split_axis=0, concat_axi...]
    dot_general x7 -> x0, matrix products: 30.2 us -> none  [the longest x1 7.46 us: expert_rows(): up = jnp.dot(rows, up_mat, preferred_element_type=jnp.float32)]
  transfers between devices with their start and end apart: 3 -> 0, of which waited for: 3 -> 0; matrix products, arithmetic and copies ran while one was open for 0% -> 0% of each run, Pallas kernels for 0% -> 0%
where the time goes in v1:
time: 127 us
  Pallas kernels  125 us (98%)
  local copies, waits for them, and re-layouts  1.72 us (1%)
    pallas_call x1, Pallas kernels, shards(): pl.pallas_call(functools.partial(layer_kernel, cfg), out_shape=jax.ShapeD...  125 us

profile of v1, /device:TPU:2, one launch (start us, length us, event | category | flops | bytes accessed | tf_op | source)
XLA Modules:
  0.0 127.1 jit_solution(7710655644042144023)
XLA Ops:
  0.0 125.4 %moe_layer.1 = bf16[64,2560]{1,0:T(8,128)(2,1)} custom-call(bf16[64,2560]{1,0:T(8,128)(2,1)} %tok_ref.1, s32[8,64]{1,0:T(8,128)} %bitcast.2, bf16[8,64]{1,0:T(8,128)(2,1)} %bitcast.3, bf16[1,2560,768]{2,1,0:T(8,128)(2,1)} %wg_hbm.1, bf16[1,2560,768]{2,1,0:T(8,128)(2,1)} %wu_hbm.1, bf16[1,768,2560]{2,1,0:T(8,128)(2,1)} %wd_hbm.1), custom_call_target="tpu_custom_call" | custom-call | tf_op jit(solution)/shard_map/moe_layer/pallas_call | solution.py:312
  125.4 1.7 %copy.8 = bf16[64,2560]{1,0:T(8,128)(2,1)} copy(bf16[64,2560]{1,0:T(8,128)(2,1)} %moe_layer.1) | data formatting | bytes 655360

commit v2 on v1

--- a/solution.py
+++ b/solution.py
@@ -11,7 +11,8 @@
 GROUPS_TOK = 4
 RING_Z = 8
 LANES = 128
-BLOCKS_CHUNK = 8
+LAGS = (1, 2, 3, 4)
+BLOCKS_CHUNK = 4
 
 
 def tile_of(size, most):
@@ -25,8 +26,8 @@
     cfg,
     tok_ref, ids_ref, gates_ref, wg_hbm, wu_hbm, wd_hbm,
     out_ref,
-    wg, wu, wd, sent, place_ref, rows, wcol, hidden, part, half_in, full_in, back, returned,
-    w_sem, a_send, a_recv, d_send, d_recv, f_send, f_recv, p_send, p_recv, q_send, q_recv, b_send, b_recv,
+    wg, wu, wd, sent, sent_gates, place_ref, rows, gates_in, packed, wcol, hidden, part, half_in, full_in, back, returned,
+    wide_sem, w_sem, a_send, a_recv, h_send, h_recv, d_send, d_recv, f_send, f_recv, g_send, g_recv, p_send, p_recv, q_send, q_recv, b_send, b_recv,
 ):
     n_group, cap, nz, nb, chunks, width, ff = cfg
     nx = n_group // nz
@@ -41,21 +42,45 @@
     my = lax.axis_index("local")
     right, left = lax.rem(my + 1, 4), lax.rem(my + 3, 4)
 
+    def lane_block(group):
+        dx, dz = lax.rem(group // nz + nx - mx, nx), lax.rem(lax.rem(group, nz) + nz - mz, nz)
+        if (nx, nz) != (4, 8):
+            return lax.rem(dx * nz + dz, nb)
+        split = jnp.minimum(lax.rem(dz, 4), 1)
+        b = (1 - split) * dx + split * (2 * lax.rem(dx, 2) + dz // 4)
+        return b
+
+    def offset(j):
+        if (nx, nz) != (4, 8):
+            return j // nz, lax.rem(j, nz)
+        c, b = j // 4, lax.rem(j, 4)
+        both = (lax.rem(c, 4) + 3) // 4
+        dx = (1 - both) * b + both * (b // 2 + 2 * (c // 4))
+        return dx, (4 - jnp.abs(c - 4)) * (1 - 2 * lax.rem(b, 2))
+
     def forth(j):
-        return lax.rem(mx + j // nz, nx) * nz + lax.rem(mz + lax.rem(j, nz), nz)
+        dx, dz = offset(j)
+        return lax.rem(mx + dx, nx) * nz + lax.rem(mz + dz + nz, nz)
 
     def origin(j):
-        return lax.rem(mx + nx - j // nz, nx) * nz + lax.rem(mz + nz - lax.rem(j, nz), nz)
+        dx, dz = offset(j)
+        return lax.rem(mx - dx + nx, nx) * nz + lax.rem(mz - dz + nz, nz)
 
     barrier = pltpu.get_barrier_semaphore()
 
-    def greet(j, carry):
-        pl.semaphore_signal(barrier, inc=1, device_id={"group": forth(j)}, device_id_type=MESH)
-        return carry
-
-    lax.fori_loop(1, n_group, greet, 0)
-    pl.semaphore_signal(barrier, inc=1, device_id={"local": right}, device_id_type=MESH)
-    pl.semaphore_signal(barrier, inc=1, device_id={"local": left}, device_id_type=MESH)
+    def at_group(dx, dz):
+        return {"group": lax.rem(mx + dx, nx) * nz + lax.rem(mz + dz, nz)}
+
+    ring = sorted({1, nz - 1})
+    near_by = [at_group(dx, 0) for dx in range(1, nx)] + [at_group(0, dz) for dz in ring]
+    near_by += [{"local": right}, {"local": left}]
+    for device in near_by:
+        pl.semaphore_signal(barrier, inc=1, device_id=device, device_id_type=MESH)
+
+    def widen(k):
+        for dz in ring:
+            pl.semaphore_signal(wide_sem.at[k], inc=1, device_id=at_group(0, dz), device_id_type=MESH)
+        pl.semaphore_wait(wide_sem.at[k], len(ring))
 
     loads = [
         pltpu.make_async_copy(hbm.at[0], vmem, w_sem.at[i])
@@ -85,9 +110,11 @@
     across = (((1,), (1,)), ((), ()))
     same_tok = jnp.where(t_row == t_col, 1.0, 0.0).astype(bf16)
     place_ref[...] = lax.dot_general(same_tok, place, across, preferred_element_type=f32).astype(bf16)
-    sent[:, width:] = lax.dot_general(
-        place, weight.astype(bf16), across, preferred_element_type=f32
-    ).astype(bf16)
+    of_slot = lax.dot_general(place, weight.astype(bf16), across, preferred_element_type=f32).astype(bf16)
+    e_row = lax.broadcasted_iota(jnp.int32, (LANES, LANES), 0)
+    e_lane = lax.broadcasted_iota(jnp.int32, (LANES, LANES), 1)
+    to_lane = jnp.where(e_lane == lane_block(e_row // 4) * 4 + lax.rem(e_row, 4), 1.0, 0.0).astype(bf16)
+    sent_gates[...] = jnp.dot(of_slot * in_group, to_lane, preferred_element_type=f32).astype(bf16)
     cols = tile_of(width, 512)
 
     def gather_cols(n, carry):
@@ -96,7 +123,7 @@
         return carry
 
     lax.fori_loop(0, width // cols, gather_cols, 0)
-    pl.semaphore_wait(barrier, n_group + 1)
+    pl.semaphore_wait(barrier, len(near_by))
 
     def block(ref, index):
         return ref.at[pl.ds(pl.multiple_of(index * cap, cap), cap), :]
@@ -112,6 +139,17 @@
             device_id_type=MESH,
         )
 
+    def dispatch_gates(j):
+        target = forth(j)
+        return pltpu.make_async_remote_copy(
+            src_ref=block(sent_gates, target),
+            dst_ref=gates_in.at[j // nb, lax.rem(j, nb)],
+            send_sem=h_send.at[j],
+            recv_sem=h_recv.at[j],
+            device_id={"group": target},
+            device_id_type=MESH,
+        )
+
     def give_back(j):
         return pltpu.make_async_remote_copy(
             src_ref=block(back.at[j // nb], lax.rem(j, nb)),
@@ -124,12 +162,20 @@
 
     own_in = pltpu.make_async_copy(block(sent, me), rows.at[0, pl.ds(0, cap), :], a_recv.at[0])
     own_in.start()
+    own_gates = pltpu.make_async_copy(block(sent_gates, me), gates_in.at[0, 0], h_recv.at[0])
+    own_gates.start()
 
     def start_dispatch(j, carry):
         dispatch(j).start()
-        return carry
-
-    lax.fori_loop(1, n_group, start_dispatch, 0)
+        dispatch_gates(j).start()
+        return carry
+
+    for k in range(nz // 2 + 1):
+        if k:
+            widen(k - 1)
+        first, last = (max(1, nx * k), nx * (k + 1)) if (nx, nz) == (4, 8) else (1, n_group if k else 1)
+        last = n_group if k == nz // 2 else last
+        lax.fori_loop(first, last, start_dispatch, 0)
 
     def copy_y(src, dst, send, recv, side):
         return pltpu.make_async_remote_copy(
@@ -150,6 +196,12 @@
         return copy_y(piece(rows, c, (n3, n1 + half)[side], half), piece(rows, c, (n2, n2 + half)[side], half),
                       f_send.at[c, side], f_recv.at[c, side], side)
 
+    def direct_weights(c, side):
+        return copy_y(packed.at[c, 0], packed.at[c, (3, 1)[side]], g_send.at[c, side], g_recv.at[c, side], side)
+
+    def onward_weights(c):
+        return copy_y(packed.at[c, 3], packed.at[c, 2], g_send.at[c, 2], g_recv.at[c, 2], 0)
+
     def far(c, side):
         return copy_y(piece(part, c, (n2, n2 + half)[side], half), half_in.at[c, side],
                       p_send.at[c, side], p_recv.at[c, side], side)
@@ -163,14 +215,16 @@
     dcols = tile_of(width, 512)
 
     def compute(c):
-        lane = lax.broadcasted_iota(jnp.int32, (4 * part_rows, LANES), 1)
-        gate_of = rows[c, :, width:].astype(f32)
-        mine = jnp.sum(jnp.where(lane == me * 4 + my, gate_of, 0.0), axis=1, keepdims=True)
-        wcol[...] = jnp.broadcast_to(mine, (4 * part_rows, LANES))
+        lane = lax.broadcasted_iota(jnp.int32, (cap, LANES), 1)
+        for r in range(4):
+            gate_of = packed[c, r].astype(f32)
+            for b in range(nb):
+                mine = jnp.sum(jnp.where(lane == b * 4 + my, gate_of, 0.0), axis=1, keepdims=True)
+                wcol[pl.ds(r * part_rows + b * cap, cap), :] = jnp.broadcast_to(mine, (cap, LANES))
 
         def up_cols(n, carry):
             at = pl.ds(pl.multiple_of(n * fcols, fcols), fcols)
-            x = rows[c, :, :width]
+            x = rows[c]
             gate = jnp.dot(x, wg[:, at], preferred_element_type=f32)
             up = jnp.dot(x, wu[:, at], preferred_element_type=f32)
             hidden[:, at] = (gate / (1.0 + jnp.exp(-gate)) * up).astype(bf16)
@@ -197,19 +251,32 @@
                 return inner
 
             lax.fori_loop(0, nb, arrived, 0)
-            direct(c, 0).start()
-            direct(c, 1).start()
-
-        @pl.when((s >= 1) & (s <= chunks))
+
+            def gates_arrived(b, inner):
+                j = c * nb + b
+                pltpu.make_async_copy(block(sent_gates, 0), gates_in.at[c, b], h_recv.at[j]).wait()
+                return inner
+
+            lax.fori_loop(0, nb, gates_arrived, 0)
+            packed[c, 0] = jnp.sum(gates_in[c].astype(f32), axis=0).astype(bf16)
+            for side in (0, 1):
+                direct(c, side).start()
+            for side in (0, 1):
+                direct_weights(c, side).start()
+
+        @pl.when((s >= LAGS[0]) & (s < chunks + LAGS[0]))
         def _():
-            c = s - 1
+            c = s - LAGS[0]
             for side in (0, 1):
                 direct(c, side).wait_recv()
                 onward(c, side).start()
-
-        @pl.when((s >= 2) & (s <= chunks + 1))
+            for side in (0, 1):
+                direct_weights(c, side).wait_recv()
+            onward_weights(c).start()
+
+        @pl.when((s >= LAGS[1]) & (s < chunks + LAGS[1]))
         def _():
-            c = s - 2
+            c = s - LAGS[1]
 
             @pl.when(c == 0)
             def _():
@@ -218,24 +285,25 @@
 
             for side in (0, 1):
                 onward(c, side).wait_recv()
+            onward_weights(c).wait_recv()
             compute(c)
             for side in (0, 1):
                 far(c, side).start()
             for side in (0, 1):
                 near(c, side, 0).start()
 
-        @pl.when((s >= 3) & (s <= chunks + 2))
+        @pl.when((s >= LAGS[2]) & (s < chunks + LAGS[2]))
         def _():
-            c = s - 3
+            c = s - LAGS[2]
             for side in (0, 1):
                 far(c, side).wait_recv()
                 at = pl.ds((n1, n3 + half)[side], half)
                 part[c, at, :] = (part[c, at, :].astype(f32) + half_in[c, side].astype(f32)).astype(bf16)
                 near(c, side, 1).start()
 
-        @pl.when(s >= 4)
+        @pl.when(s >= LAGS[3])
         def _():
-            c = s - 4
+            c = s - LAGS[3]
             for which in (0, 1):
                 for side in (0, 1):
                     near(c, side, which).wait_recv()
@@ -262,21 +330,24 @@
 
         return carry
 
-    lax.fori_loop(0, chunks + 4, step, 0)
+    lax.fori_loop(0, chunks + LAGS[3], step, 0)
 
     def sends_done(c, carry):
         for side in (0, 1):
             direct(c, side).wait_send()
+            direct_weights(c, side).wait_send()
             onward(c, side).wait_send()
             far(c, side).wait_send()
             near(c, side, 0).wait_send()
             near(c, side, 1).wait_send()
+        onward_weights(c).wait_send()
         return carry
 
     lax.fori_loop(0, chunks, sends_done, 0)
 
     def blocks_done(j, carry):
         dispatch(j).wait_send()
+        dispatch_gates(j).wait_send()
         give_back(j).wait_send()
         return carry
 
@@ -318,9 +389,12 @@
             pltpu.VMEM((width, ff), bf16),
             pltpu.VMEM((width, ff), bf16),
             pltpu.VMEM((ff, width), bf16),
-            pltpu.VMEM((n_group * cap, width + LANES), bf16),
+            pltpu.VMEM((n_group * cap, width), bf16),
+            pltpu.VMEM((n_group * cap, LANES), bf16),
             pltpu.VMEM((n_tok, n_group * cap), bf16),
-            pltpu.VMEM((chunks, 4 * n1, width + LANES), bf16),
+            pltpu.VMEM((chunks, 4 * n1, width), bf16),
+            pltpu.VMEM((chunks, nb, cap, LANES), bf16),
+            pltpu.VMEM((chunks, 4, cap, LANES), bf16),
             pltpu.VMEM((4 * n1, LANES), jnp.float32),
             pltpu.VMEM((4 * n1, ff), bf16),
             pltpu.VMEM((chunks, 4 * n1, width), bf16),
@@ -328,10 +402,13 @@
             pltpu.VMEM((chunks, 2, n1, width), bf16),
             pltpu.VMEM((chunks, n1, width), bf16),
             pltpu.VMEM((n_group * cap, width), bf16),
+            pltpu.SemaphoreType.REGULAR((ring_z // 2,)),
             dma((3,)),
+            dma((n_group,)), dma((n_group,)),
             dma((n_group,)), dma((n_group,)),
             dma((chunks, 2)), dma((chunks, 2)),
             dma((chunks, 2)), dma((chunks, 2)),
+            dma((chunks, 3)), dma((chunks, 3)),
             dma((chunks, 2)), dma((chunks, 2)),
             dma((chunks, 4)), dma((chunks, 4)),
             dma((n_group,)), dma((n_group,)),

time: 127 us -> 117 us (0.921)
  Pallas kernels: 125 us -> 115 us
    pallas_call x1, Pallas kernels: 125 us -> 115 us  [shards(): pl.pallas_call(functools.partial(layer_kernel, cfg), out_shape=jax.ShapeD...]
where the time goes in v2:
time: 117 us; the launch traced here: 116 us
  Pallas kernels  115 us (98%)
  local copies, waits for them, and re-layouts  1.72 us (1%)
    pallas_call x1, Pallas kernels, shards(): pl.pallas_call(functools.partial(layer_kernel, cfg), out_shape=jax.ShapeD...  115 us

profile of v2, /device:TPU:2, one launch (start us, length us, event | category | flops | bytes accessed | tf_op | source)
XLA Modules:
  0.0 116.5 jit_solution(2467883850074614825)
XLA Ops:
  0.0 114.7 %moe_layer.1 = bf16[64,2560]{1,0:T(8,128)(2,1)} custom-call(bf16[64,2560]{1,0:T(8,128)(2,1)} %tok_ref.1, s32[8,64]{1,0:T(8,128)} %bitcast.2, bf16[8,64]{1,0:T(8,128)(2,1)} %bitcast.3, bf16[1,2560,768]{2,1,0:T(8,128)(2,1)} %wg_hbm.1, bf16[1,2560,768]{2,1,0:T(8,128)(2,1)} %wu_hbm.1, bf16[1,768,2560]{2,1,0:T(8,128)(2,1)} %wd_hbm.1), custom_call_target="tpu_custom_call" | custom-call | tf_op jit(solution)/shard_map/moe_layer/pallas_call | solution.py:383
  114.7 1.7 %copy.8 = bf16[64,2560]{1,0:T(8,128)(2,1)} copy(bf16[64,2560]{1,0:T(8,128)(2,1)} %moe_layer.1) | data formatting | bytes 655360

commit v3 on v2

--- a/solution.py
+++ b/solution.py
@@ -11,7 +11,8 @@
 GROUPS_TOK = 4
 RING_Z = 8
 LANES = 128
-LAGS = (1, 2, 3, 4)
+PREPARE = (1, 2)
+LAGS = (1, 3, 4, 5)
 BLOCKS_CHUNK = 4
 
 
@@ -26,8 +27,8 @@
     cfg,
     tok_ref, ids_ref, gates_ref, wg_hbm, wu_hbm, wd_hbm,
     out_ref,
-    wg, wu, wd, sent, sent_gates, place_ref, rows, gates_in, packed, wcol, hidden, part, half_in, full_in, back, returned,
-    wide_sem, w_sem, a_send, a_recv, h_send, h_recv, d_send, d_recv, f_send, f_recv, g_send, g_recv, p_send, p_recv, q_send, q_recv, b_send, b_recv,
+    wg, wu, wd, route_in, tok_in, places, sent, sent_gates, place_ref, rows, gates_in, packed, wcol, hidden, part, half_in, full_in, back, returned,
+    wide_sem, w_sem, t_send, t_recv, s_send, s_recv, a_send, a_recv, h_send, h_recv, d_send, d_recv, f_send, f_recv, g_send, g_recv, p_send, p_recv, q_send, q_recv, b_send, b_recv,
 ):
     n_group, cap, nz, nb, chunks, width, ff = cfg
     nx = n_group // nz
@@ -42,6 +43,23 @@
     my = lax.axis_index("local")
     right, left = lax.rem(my + 1, 4), lax.rem(my + 3, 4)
 
+    full_size = (nx, nz) == (4, 8) and nb == 4
+
+    def chunk_of(p):
+        return lax.rem(p + 2, chunks) if full_size else p
+
+    def is_far(c):
+        return (c >= 2) & (c <= 6) if full_size else c >= 1
+
+    n_near = 3 if full_size else 1
+    far_blocks = (2 * nb, 7 * nb) if full_size else (nb, n_group)
+
+    def near_chunk(i):
+        return i + 5 * (i // 2) if full_size else i
+
+    def near_index(c):
+        return c - 5 * (c // 7) if full_size else c
+
     def lane_block(group):
         dx, dz = lax.rem(group // nz + nx - mx, nx), lax.rem(lax.rem(group, nz) + nz - mz, nz)
         if (nx, nz) != (4, 8):
@@ -77,9 +95,11 @@
     for device in near_by:
         pl.semaphore_signal(barrier, inc=1, device_id=device, device_id_type=MESH)
 
-    def widen(k):
+    def tell(k):
         for dz in ring:
             pl.semaphore_signal(wide_sem.at[k], inc=1, device_id=at_group(0, dz), device_id_type=MESH)
+
+    def hear(k):
         pl.semaphore_wait(wide_sem.at[k], len(ring))
 
     loads = [
@@ -89,41 +109,51 @@
     for load in loads:
         load.start()
 
-    expert_at = lax.broadcasted_iota(jnp.int32, (LANES, n_tok), 0)
-    hit = jnp.zeros((LANES, n_tok), f32)
-    weight = jnp.zeros((LANES, n_tok), f32)
-    for k in range(ids_ref.shape[0]):
-        same = ids_ref[k : k + 1, :] == expert_at
-        hit = jnp.where(same, 1.0, hit)
-        weight = jnp.where(same, gates_ref[k : k + 1, :].astype(f32), weight)
+    top = ids_ref.shape[0]
+    route_in[0] = jnp.zeros_like(route_in[0])
+    route_in[0, pl.ds(0, top), pl.ds(0, n_tok)] = ids_ref[...].astype(f32).astype(bf16)
+    route_in[0, pl.ds(top, top), pl.ds(0, n_tok)] = gates_ref[...]
+
+    expert_at = lax.broadcasted_iota(jnp.int32, (LANES, n_tok), 0).astype(f32)
     slot_at = lax.broadcasted_iota(jnp.int32, (slots, LANES), 0)
     of_expert = lax.broadcasted_iota(jnp.int32, (slots, LANES), 1)
     in_group = jnp.where(slot_at // cap == of_expert // 4, 1.0, 0.0).astype(bf16)
-    count = jnp.dot(in_group, hit.astype(bf16), preferred_element_type=f32)
-    member = jnp.where(count > 0.5, 1.0, 0.0)
     t_row = lax.broadcasted_iota(jnp.int32, (n_tok, n_tok), 0)
     t_col = lax.broadcasted_iota(jnp.int32, (n_tok, n_tok), 1)
     before = jnp.where(t_row < t_col, 1.0, 0.0).astype(bf16)
-    rank = jnp.dot(member.astype(bf16), before, preferred_element_type=f32)
     slot_rank = lax.rem(lax.broadcasted_iota(jnp.int32, (slots, n_tok), 0), cap).astype(f32)
-    place = jnp.where((count > 0.5) & (rank == slot_rank), 1.0, 0.0).astype(bf16)
     across = (((1,), (1,)), ((), ()))
     same_tok = jnp.where(t_row == t_col, 1.0, 0.0).astype(bf16)
-    place_ref[...] = lax.dot_general(same_tok, place, across, preferred_element_type=f32).astype(bf16)
-    of_slot = lax.dot_general(place, weight.astype(bf16), across, preferred_element_type=f32).astype(bf16)
     e_row = lax.broadcasted_iota(jnp.int32, (LANES, LANES), 0)
     e_lane = lax.broadcasted_iota(jnp.int32, (LANES, LANES), 1)
     to_lane = jnp.where(e_lane == lane_block(e_row // 4) * 4 + lax.rem(e_row, 4), 1.0, 0.0).astype(bf16)
-    sent_gates[...] = jnp.dot(of_slot * in_group, to_lane, preferred_element_type=f32).astype(bf16)
     cols = tile_of(width, 512)
 
-    def gather_cols(n, carry):
-        at = pl.ds(pl.multiple_of(n * cols, cols), cols)
-        sent[:, at] = jnp.dot(place, tok_ref[:, at], preferred_element_type=f32).astype(bf16)
-        return carry
-
-    lax.fori_loop(0, width // cols, gather_cols, 0)
-    pl.semaphore_wait(barrier, len(near_by))
+    def route(r):
+        hit = jnp.zeros((LANES, n_tok), f32)
+        weight = jnp.zeros((LANES, n_tok), f32)
+        for k in range(top):
+            same = route_in[r, k : k + 1, :n_tok].astype(f32) == expert_at
+            hit = jnp.where(same, 1.0, hit)
+            weight = jnp.where(same, route_in[r, top + k : top + k + 1, :n_tok].astype(f32), weight)
+        count = jnp.dot(in_group, hit.astype(bf16), preferred_element_type=f32)
+        member = jnp.where(count > 0.5, 1.0, 0.0)
+        rank = jnp.dot(member.astype(bf16), before, preferred_element_type=f32)
+        place = jnp.where((count > 0.5) & (rank == slot_rank), 1.0, 0.0).astype(bf16)
+        places[r] = place
+        of_slot = lax.dot_general(place, weight.astype(bf16), across, preferred_element_type=f32).astype(bf16)
+        moved = jnp.dot(of_slot * in_group, to_lane, preferred_element_type=f32)
+        sent_gates[:, r] = moved.reshape(n_group, cap, LANES).astype(bf16)
+        return place
+
+    def fill(r):
+        def gather_cols(n, carry):
+            at = pl.ds(pl.multiple_of(n * cols, cols), cols)
+            tok = tok_ref[:, at] if r == 0 else tok_in[r, :, at]
+            sent[r, :, at] = jnp.dot(places[r], tok, preferred_element_type=f32).astype(bf16)
+            return carry
+
+        lax.fori_loop(0, width // cols, gather_cols, 0)
 
     def block(ref, index):
         return ref.at[pl.ds(pl.multiple_of(index * cap, cap), cap), :]
@@ -131,7 +161,7 @@
     def dispatch(j):
         target = forth(j)
         return pltpu.make_async_remote_copy(
-            src_ref=block(sent, target),
+            src_ref=block(sent.at[0], target),
             dst_ref=block(rows.at[j // nb], lax.rem(j, nb)),
             send_sem=a_send.at[j],
             recv_sem=a_recv.at[j],
@@ -139,16 +169,47 @@
             device_id_type=MESH,
         )
 
-    def dispatch_gates(j):
+    def gates_copy(j, far_chunk):
         target = forth(j)
+        at = (j // nb, lax.rem(j, nb)) + ((0,) if far_chunk else ())
         return pltpu.make_async_remote_copy(
-            src_ref=block(sent_gates, target),
-            dst_ref=gates_in.at[j // nb, lax.rem(j, nb)],
+            src_ref=sent_gates.at[target, 0] if far_chunk else sent_gates.at[target],
+            dst_ref=gates_in.at[at],
             send_sem=h_send.at[j],
             recv_sem=h_recv.at[j],
             device_id={"group": target},
             device_id_type=MESH,
         )
+
+    def near_copy(i, r):
+        j = near_chunk(i // nb) * nb + lax.rem(i, nb)
+        target = forth(j)
+        return pltpu.make_async_remote_copy(
+            src_ref=block(sent.at[r], target),
+            dst_ref=block(rows.at[j // nb], r * nb + lax.rem(j, nb)),
+            send_sem=s_send.at[i, r],
+            recv_sem=s_recv.at[i, r],
+            device_id={"group": target},
+            device_id_type=MESH,
+        )
+
+    def near_rows(r):
+        pltpu.make_async_copy(block(sent.at[r], me), block(rows.at[0], r * nb), s_recv.at[0, r]).start()
+
+        def one(i, carry):
+            near_copy(i, r).start()
+            return carry
+
+        lax.fori_loop(1, n_near * nb, one, 0)
+
+    def near_gates():
+        pltpu.make_async_copy(sent_gates.at[me], gates_in.at[0, 0], h_recv.at[0]).start()
+
+        def one(i, carry):
+            gates_copy(near_chunk(i // nb) * nb + lax.rem(i, nb), False).start()
+            return carry
+
+        lax.fori_loop(1, n_near * nb, one, 0)
 
     def give_back(j):
         return pltpu.make_async_remote_copy(
@@ -160,28 +221,55 @@
             device_id_type=MESH,
         )
 
-    own_in = pltpu.make_async_copy(block(sent, me), rows.at[0, pl.ds(0, cap), :], a_recv.at[0])
-    own_in.start()
-    own_gates = pltpu.make_async_copy(block(sent_gates, me), gates_in.at[0, 0], h_recv.at[0])
-    own_gates.start()
-
-    def start_dispatch(j, carry):
-        dispatch(j).start()
-        dispatch_gates(j).start()
-        return carry
-
-    for k in range(nz // 2 + 1):
-        if k:
-            widen(k - 1)
-        first, last = (max(1, nx * k), nx * (k + 1)) if (nx, nz) == (4, 8) else (1, n_group if k else 1)
-        last = n_group if k == nz // 2 else last
-        lax.fori_loop(first, last, start_dispatch, 0)
-
     def copy_y(src, dst, send, recv, side):
         return pltpu.make_async_remote_copy(
             src_ref=src, dst_ref=dst, send_sem=send, recv_sem=recv,
             device_id={"local": right if side == 0 else left}, device_id_type=MESH,
         )
+
+    hn = n_tok // 2
+
+    def tile_direct(side):
+        return copy_y(route_in.at[0], route_in.at[(3, 1)[side]], t_send.at[side], t_recv.at[side], side)
+
+    def tile_onward():
+        return copy_y(route_in.at[3], route_in.at[2], t_send.at[2], t_recv.at[2], 0)
+
+    def tok_direct(side, second):
+        at = pl.ds(hn if (side == 0) == second else 0, hn)
+        k = 3 + 2 * side + int(second)
+        return copy_y(tok_ref.at[at, :], tok_in.at[(3, 1)[side], at, :], t_send.at[k], t_recv.at[k], side)
+
+    def tok_onward(side):
+        at = pl.ds((0, hn)[side], hn)
+        return copy_y(tok_in.at[(3, 1)[side], at, :], tok_in.at[2, at, :], t_send.at[7 + side], t_recv.at[7 + side], side)
+
+    pl.semaphore_wait(barrier, len(near_by))
+    for side in (0, 1):
+        tile_direct(side).start()
+    for side in (0, 1):
+        tok_direct(side, False).start()
+    for side in (0, 1):
+        tok_direct(side, True).start()
+    tell(0)
+    place_ref[...] = lax.dot_general(same_tok, route(0), across, preferred_element_type=f32).astype(bf16)
+    fill(0)
+
+    def start_far(j, carry):
+        dispatch(j).start()
+        gates_copy(j, True).start()
+        return carry
+
+    done = far_blocks[0]
+    for k in range(nz // 2):
+        hear(k)
+        if k + 1 < nz // 2:
+            tell(k + 1)
+        reach = far_blocks[1] if k + 1 == nz // 2 else nb * (k + 2) if full_size else done
+        if reach > done:
+            lax.fori_loop(done, reach, start_far, 0)
+        done = max(done, reach)
+    near_rows(0)
 
     def piece(ref, c, begin, size):
         return ref.at[c, pl.ds(begin, size), :]
@@ -241,32 +329,39 @@
         lax.fori_loop(0, width // dcols, down_cols, 0)
 
     def step(s, carry):
-        @pl.when(s < chunks)
-        def _():
-            c = s
+        first = chunk_of(jnp.minimum(s, chunks - 1))
+
+        @pl.when((s < chunks) & is_far(first))
+        def _():
+            c = first
 
             def arrived(b, inner):
                 j = c * nb + b
-                pltpu.make_async_copy(block(sent, 0), block(rows.at[c], b), a_recv.at[j]).wait()
+                pltpu.make_async_copy(block(sent.at[0], 0), block(rows.at[c], b), a_recv.at[j]).wait()
+                pltpu.make_async_copy(sent_gates.at[0, 0], gates_in.at[c, b, 0], h_recv.at[j]).wait()
                 return inner
 
             lax.fori_loop(0, nb, arrived, 0)
-
-            def gates_arrived(b, inner):
-                j = c * nb + b
-                pltpu.make_async_copy(block(sent_gates, 0), gates_in.at[c, b], h_recv.at[j]).wait()
-                return inner
-
-            lax.fori_loop(0, nb, gates_arrived, 0)
-            packed[c, 0] = jnp.sum(gates_in[c].astype(f32), axis=0).astype(bf16)
+            packed[c, 0] = jnp.sum(gates_in[c, :, 0].astype(f32), axis=0).astype(bf16)
             for side in (0, 1):
                 direct(c, side).start()
             for side in (0, 1):
                 direct_weights(c, side).start()
 
-        @pl.when((s >= LAGS[0]) & (s < chunks + LAGS[0]))
-        def _():
-            c = s - LAGS[0]
+        @pl.when(s == 0)
+        def _():
+            for side in (0, 1):
+                tok_direct(side, False).wait_recv()
+                tok_onward(side).start()
+            for side in (0, 1):
+                tile_direct(side).wait_recv()
+            tile_onward().start()
+
+        second = chunk_of(jnp.clip(s - LAGS[0], 0, chunks - 1))
+
+        @pl.when((s >= LAGS[0]) & (s < chunks + LAGS[0]) & is_far(second))
+        def _():
+            c = second
             for side in (0, 1):
                 direct(c, side).wait_recv()
                 onward(c, side).start()
@@ -274,18 +369,53 @@
                 direct_weights(c, side).wait_recv()
             onward_weights(c).start()
 
+        @pl.when(s == PREPARE[0])
+        def _():
+            for side in (0, 1):
+                tok_direct(side, True).wait_recv()
+                r = (3, 1)[side]
+                route(r)
+                fill(r)
+                near_rows(r)
+
+        @pl.when(s == PREPARE[1])
+        def _():
+            for side in (0, 1):
+                tok_onward(side).wait_recv()
+            tile_onward().wait_recv()
+            route(2)
+            fill(2)
+            near_rows(2)
+            near_gates()
+
         @pl.when((s >= LAGS[1]) & (s < chunks + LAGS[1]))
         def _():
-            c = s - LAGS[1]
-
-            @pl.when(c == 0)
+            c = chunk_of(s - LAGS[1])
+
+            @pl.when(s == LAGS[1])
             def _():
                 for load in loads:
                     load.wait()
 
-            for side in (0, 1):
-                onward(c, side).wait_recv()
-            onward_weights(c).wait_recv()
+            @pl.when(is_far(c))
+            def _():
+                for side in (0, 1):
+                    onward(c, side).wait_recv()
+                onward_weights(c).wait_recv()
+
+            @pl.when(jnp.logical_not(is_far(c)))
+            def _():
+                def arrived(b, inner):
+                    for r in range(4):
+                        pltpu.make_async_copy(
+                            block(sent.at[r], 0), block(rows.at[c], r * nb + b), s_recv.at[near_index(c) * nb + b, r]
+                        ).wait()
+                    pltpu.make_async_copy(sent_gates.at[0], gates_in.at[c, b], h_recv.at[c * nb + b]).wait()
+                    return inner
+
+                lax.fori_loop(0, nb, arrived, 0)
+                packed[c] = jnp.sum(gates_in[c].astype(f32), axis=0).astype(bf16)
+
             compute(c)
             for side in (0, 1):
                 far(c, side).start()
@@ -294,7 +424,7 @@
 
         @pl.when((s >= LAGS[2]) & (s < chunks + LAGS[2]))
         def _():
-            c = s - LAGS[2]
+            c = chunk_of(s - LAGS[2])
             for side in (0, 1):
                 far(c, side).wait_recv()
                 at = pl.ds((n1, n3 + half)[side], half)
@@ -303,7 +433,7 @@
 
         @pl.when(s >= LAGS[3])
         def _():
-            c = s - LAGS[3]
+            c = chunk_of(s - LAGS[3])
             for which in (0, 1):
                 for side in (0, 1):
                     near(c, side, which).wait_recv()
@@ -333,21 +463,44 @@
     lax.fori_loop(0, chunks + LAGS[3], step, 0)
 
     def sends_done(c, carry):
+        @pl.when(is_far(c))
+        def _():
+            for side in (0, 1):
+                direct(c, side).wait_send()
+                direct_weights(c, side).wait_send()
+                onward(c, side).wait_send()
+            onward_weights(c).wait_send()
+
         for side in (0, 1):
-            direct(c, side).wait_send()
-            direct_weights(c, side).wait_send()
-            onward(c, side).wait_send()
             far(c, side).wait_send()
             near(c, side, 0).wait_send()
             near(c, side, 1).wait_send()
-        onward_weights(c).wait_send()
         return carry
 
     lax.fori_loop(0, chunks, sends_done, 0)
+    for side in (0, 1):
+        tile_direct(side).wait_send()
+        tok_direct(side, False).wait_send()
+        tok_direct(side, True).wait_send()
+        tok_onward(side).wait_send()
+    tile_onward().wait_send()
+
+    def far_sent(j, carry):
+        dispatch(j).wait_send()
+        gates_copy(j, True).wait_send()
+        return carry
+
+    lax.fori_loop(*far_blocks, far_sent, 0)
+
+    def near_sent(i, carry):
+        for r in range(4):
+            near_copy(i, r).wait_send()
+        gates_copy(near_chunk(i // nb) * nb + lax.rem(i, nb), False).wait_send()
+        return carry
+
+    lax.fori_loop(1, n_near * nb, near_sent, 0)
 
     def blocks_done(j, carry):
-        dispatch(j).wait_send()
-        dispatch_gates(j).wait_send()
         give_back(j).wait_send()
         return carry
 
@@ -389,11 +542,14 @@
             pltpu.VMEM((width, ff), bf16),
             pltpu.VMEM((width, ff), bf16),
             pltpu.VMEM((ff, width), bf16),
-            pltpu.VMEM((n_group * cap, width), bf16),
-            pltpu.VMEM((n_group * cap, LANES), bf16),
+            pltpu.VMEM((4, 2 * expert_ids.shape[1], LANES), bf16),
+            pltpu.VMEM((4, n_tok, width), bf16),
+            pltpu.VMEM((4, n_group * cap, n_tok), bf16),
+            pltpu.VMEM((4, n_group * cap, width), bf16),
+            pltpu.VMEM((n_group, 4, cap, LANES), bf16),
             pltpu.VMEM((n_tok, n_group * cap), bf16),
             pltpu.VMEM((chunks, 4 * n1, width), bf16),
-            pltpu.VMEM((chunks, nb, cap, LANES), bf16),
+            pltpu.VMEM((chunks, nb, 4, cap, LANES), bf16),
             pltpu.VMEM((chunks, 4, cap, LANES), bf16),
             pltpu.VMEM((4 * n1, LANES), jnp.float32),
             pltpu.VMEM((4 * n1, ff), bf16),
@@ -404,6 +560,8 @@
             pltpu.VMEM((n_group * cap, width), bf16),
             pltpu.SemaphoreType.REGULAR((ring_z // 2,)),
             dma((3,)),
+            dma((9,)), dma((9,)),
+            dma((3 * nb, 4)), dma((3 * nb, 4)),
             dma((n_group,)), dma((n_group,)),
             dma((n_group,)), dma((n_group,)),
             dma((chunks, 2)), dma((chunks, 2)),

time: 117 us -> 112 us (0.957)
  Pallas kernels: 115 us -> 110 us
    pallas_call x1, Pallas kernels: 115 us -> 110 us  [shards(): pl.pallas_call(functools.partial(layer_kernel, cfg), out_shape=jax.ShapeD...]
where the time goes in v3:
time: 112 us; the launch traced here: 111 us
  Pallas kernels  110 us (98%)
  local copies, waits for them, and re-layouts  1.72 us (2%)
    pallas_call x1, Pallas kernels, shards(): pl.pallas_call(functools.partial(layer_kernel, cfg), out_shape=jax.ShapeD...  110 us

profile of v3, /device:TPU:2, one launch (start us, length us, event | category | flops | bytes accessed | tf_op | source)
XLA Modules:
  0.0 111.4 jit_solution(16237341133471806592)
XLA Ops:
  0.0 109.7 %moe_layer.1 = bf16[64,2560]{1,0:T(8,128)(2,1)} custom-call(bf16[64,2560]{1,0:T(8,128)(2,1)} %tok_ref.1, s32[8,64]{1,0:T(8,128)} %bitcast.2, bf16[8,64]{1,0:T(8,128)(2,1)} %bitcast.3, bf16[1,2560,768]{2,1,0:T(8,128)(2,1)} %wg_hbm.1, bf16[1,2560,768]{2,1,0:T(8,128)(2,1)} %wu_hbm.1, bf16[1,768,2560]{2,1,0:T(8,128)(2,1)} %wd_hbm.1), custom_call_target="tpu_custom_call" | custom-call | tf_op jit(solution)/shard_map/moe_layer/pallas_call | solution.py:536
  109.7 1.7 %copy.8 = bf16[64,2560]{1,0:T(8,128)(2,1)} copy(bf16[64,2560]{1,0:T(8,128)(2,1)} %moe_layer.1) | data formatting | bytes 655360

commit v4 on v3

--- a/solution.py
+++ b/solution.py
@@ -72,9 +72,10 @@
         if (nx, nz) != (4, 8):
             return j // nz, lax.rem(j, nz)
         c, b = j // 4, lax.rem(j, 4)
-        both = (lax.rem(c, 4) + 3) // 4
-        dx = (1 - both) * b + both * (b // 2 + 2 * (c // 4))
-        return dx, (4 - jnp.abs(c - 4)) * (1 - 2 * lax.rem(b, 2))
+        both = (lax.rem(c, 6) + 5) // 6
+        dx = (1 - both) * b + both * (b // 2 + 2 * lax.rem(c, 2) * ((c + 2) // 5))
+        away = (c + 2) // 2 - (7 - c) // 7 - 3 * (c // 7)
+        return dx, away * (1 - 2 * lax.rem(b, 2))
 
     def forth(j):
         dx, dz = offset(j)
@@ -253,6 +254,9 @@
         tok_direct(side, True).start()
     tell(0)
     place_ref[...] = lax.dot_general(same_tok, route(0), across, preferred_element_type=f32).astype(bf16)
+    hear(0)
+    if nz // 2 > 1:
+        tell(1)
     fill(0)
 
     def start_far(j, carry):
@@ -262,10 +266,11 @@
 
     done = far_blocks[0]
     for k in range(nz // 2):
-        hear(k)
-        if k + 1 < nz // 2:
-            tell(k + 1)
-        reach = far_blocks[1] if k + 1 == nz // 2 else nb * (k + 2) if full_size else done
+        if k:
+            hear(k)
+            if k + 1 < nz // 2:
+                tell(k + 1)
+        reach = far_blocks[1] if k + 1 == nz // 2 else 2 * nb * (k + 1) if full_size else done
         if reach > done:
             lax.fori_loop(done, reach, start_far, 0)
         done = max(done, reach)

time: 112 us -> 109 us (0.973)
  Pallas kernels: 110 us -> 107 us
    pallas_call x1, Pallas kernels: 110 us -> 107 us  [shards(): pl.pallas_call(functools.partial(layer_kernel, cfg), out_shape=jax.ShapeD...]
where the time goes in v4:
time: 109 us
  Pallas kernels  107 us (98%)
  local copies, waits for them, and re-layouts  1.72 us (2%)
    pallas_call x1, Pallas kernels, shards(): pl.pallas_call(functools.partial(layer_kernel, cfg), out_shape=jax.ShapeD...  107 us

profile of v4, /device:TPU:2, one launch (start us, length us, event | category | flops | bytes accessed | tf_op | source)
XLA Modules:
  0.0 108.7 jit_solution(9160898645172364887)
XLA Ops:
  0.0 107.0 %moe_layer.1 = bf16[64,2560]{1,0:T(8,128)(2,1)} custom-call(bf16[64,2560]{1,0:T(8,128)(2,1)} %tok_ref.1, s32[8,64]{1,0:T(8,128)} %bitcast.2, bf16[8,64]{1,0:T(8,128)(2,1)} %bitcast.3, bf16[1,2560,768]{2,1,0:T(8,128)(2,1)} %wg_hbm.1, bf16[1,2560,768]{2,1,0:T(8,128)(2,1)} %wu_hbm.1, bf16[1,768,2560]{2,1,0:T(8,128)(2,1)} %wd_hbm.1), custom_call_target="tpu_custom_call" | custom-call | tf_op jit(solution)/shard_map/moe_layer/pallas_call | solution.py:541
  107.0 1.7 %copy.8 = bf16[64,2560]{1,0:T(8,128)(2,1)} copy(bf16[64,2560]{1,0:T(8,128)(2,1)} %moe_layer.1) | data formatting | bytes 655360
